TPU v7x, 32 devices: a whole 2x2x4 slice. The times are simulated.
32 devices in a mesh: blk: 4 (over z), grp: 8 (over y, x, core).
Axes of the slice: x: 2, y: 2, z: 4, core: 2. Of those that a mesh axis runs over, the one named last changes fastest.
Arguments:
- basis: bfloat16 [8, 512, 1152], P('grp', 'blk'), may hold values from -6 to 6
- coeffs: bfloat16 [2, 1152, 768], replicated, may hold values from -0.1875 to 0.1875
- stiff_blocks: bfloat16 [8, 4, 4, 128, 128], P('grp', 'blk'), as said below
- mass_blocks: bfloat16 [8, 4, 4, 128, 128], P('grp', 'blk'), as said below
- block_cols: int32 [8, 4, 4], P('grp', 'blk'), may hold values from 0 to 3
Outputs:
- basis_out: bfloat16 [8, 512, 1152], P('grp', 'blk')
- ritz_value: float32 [384], replicated
- gram: float32 [1152, 2, 1152], P('grp', None, 'blk')
Inputs may be any that keep to these rules, and one draw needn't show every extreme that they name: block_cols names row blocks of the same substructure. `mass_blocks`: real-valued blocks of order 1 / sqrt(512). `stiff_blocks`: real-valued blocks, of larger size than the mass blocks.
All inputs are finite; a program needn't handle non-finite values.
Results may differ from a plain program's by a relative error of at most 0.02.
Values may be sent and summed in bfloat16 or wider, within the bound.
No kernel may reach another device: no remote copies, remote signals or barrier semaphores. Data moves between devices by JAX's collectives and lax.ppermute only.
A program may use at most 64 MiB of HBM per device.

v0:
```python
import jax
import jax.numpy as jnp
from jax import lax
from jax.sharding import PartitionSpec as P

epsilon = 1e-06


def apply_pair(stiff, mass, cols, field, final):
    columns = field.shape[1]
    block_rows, slots = cols.shape
    edge = stiff.shape[-1]
    own_blocks = field.reshape(block_rows, edge, columns)
    wanted = cols.reshape(-1)

    def take_blocks(arrived):
        arrived_count = arrived.shape[0]
        ident = jnp.arange(arrived_count, dtype=jnp.int32)
        selector = (wanted[:, None] == ident[None, :]).astype(jnp.bfloat16)
        taken = jnp.dot(
            selector, arrived.reshape(arrived_count, -1), preferred_element_type=jnp.float32
        )
        return taken.astype(jnp.bfloat16)

    if final:
        gathered = take_blocks(lax.all_gather(own_blocks, "blk", axis=0, tiled=True))
    else:
        gathered = take_blocks(lax.all_gather(own_blocks, "blk", axis=0, tiled=True))
    gathered = gathered.reshape(block_rows, slots, edge, columns)
    contract = (((1, 3), (1, 2)), ((0,), (0,)))
    stiff_out = lax.dot_general(stiff, gathered, contract, preferred_element_type=jnp.float32)
    mass_out = lax.dot_general(mass, gathered, contract, preferred_element_type=jnp.float32)
    return (
        stiff_out.reshape(block_rows * edge, columns),
        mass_out.reshape(block_rows * edge, columns),
    )


def body(basis, coeffs, stiff_blocks, mass_blocks, block_cols):
    stiff = stiff_blocks[0]
    mass = mass_blocks[0]
    cols = block_cols[0]
    current = basis[0]
    rows_here, columns = current.shape
    mode_count = columns // 3
    total_rows = rows_here * lax.axis_size("blk") * lax.axis_size("grp")
    for sweep in range(coeffs.shape[0]):
        turned = jnp.dot(current, coeffs[sweep], preferred_element_type=jnp.float32).astype(
            jnp.bfloat16
        )
        next_modes = turned[:, :mode_count]
        next_history = turned[:, mode_count:]
        stiff_x, mass_x = apply_pair(stiff, mass, cols, next_modes, False)
        numerator, denominator = lax.psum(
            (jnp.sum(stiff_x * mass_x, axis=0), jnp.sum(mass_x * mass_x, axis=0)), ("blk", "grp")
        )
        ritz_value = numerator / (denominator + epsilon)
        residual = stiff_x - ritz_value * mass_x
        resid_sum = lax.psum(jnp.sum(residual * residual, axis=0), ("blk", "grp"))
        next_search = (residual * lax.rsqrt(resid_sum / total_rows + epsilon)).astype(jnp.bfloat16)
        current = jnp.concatenate([next_modes, next_search, next_history], axis=1)
    stiff_rest, mass_rest = apply_pair(stiff, mass, cols, current[:, mode_count:], True)
    stiff_all = jnp.concatenate(
        [stiff_x.astype(jnp.bfloat16), stiff_rest.astype(jnp.bfloat16)], axis=1
    )
    mass_all = jnp.concatenate(
        [mass_x.astype(jnp.bfloat16), mass_rest.astype(jnp.bfloat16)], axis=1
    )
    inner = (((0,), (0,)), ((), ()))
    gram_stiff = lax.dot_general(current, stiff_all, inner, preferred_element_type=jnp.float32)
    gram_mass = lax.dot_general(current, mass_all, inner, preferred_element_type=jnp.float32)
    by_group = lax.psum_scatter(
        jnp.stack([gram_stiff, gram_mass], axis=1).astype(jnp.bfloat16),
        "grp",
        scatter_dimension=0,
        tiled=True,
    )
    gram = lax.psum_scatter(by_group, "blk", scatter_dimension=2, tiled=True).astype(jnp.float32)
    return (current[None], ritz_value, gram)


def solution(mesh):
    in_specs = (
        P("grp", "blk", None),
        P(),
        P("grp", "blk", None, None, None),
        P("grp", "blk", None, None, None),
        P("grp", "blk", None),
    )
    out_specs = (P("grp", "blk", None), P(), P("grp", None, "blk"))
    return jax.shard_map(body, mesh=mesh, in_specs=in_specs, out_specs=out_specs, check_vma=False)
```

profile of v0, /device:TPU:0, one launch (start us, length us, event | category | flops | bytes accessed | tf_op | source)
XLA Modules:
  0.0 328.8 jit_solution(17541428477707894250)
XLA Ops:
  7.2 0.0 copy-start
  7.2 0.0 copy-start.4
  7.2 0.0 copy-start.2
  7.2 0.0 copy-start.1
  7.2 0.0 reduce-scatter.5.cloned.1.call-start
  7.3 0.9 copy-done
  8.1 1.9 fusion.8
  10.1 16.2 %all-gather = bf16[512,384]{1,0:T(8,128)(2,1)S(1)} all-gather(bf16[128,384]{1,0:T(8,128)(2,1)S(1)} %get-tuple-element.22), channel_id=2, replica_groups=mesh['blk'=4,'grp'=8] {'blk'}, dimensions={0}, use_global_device_ids=true | all-gather | bytes 491520 | tf_op jit(solution)/shard_map/all_gather | solution.py:28
  26.3 0.1 reshape.85
  26.5 0.0 copy-done.4
  26.5 0.4 convolution_convert_fusion.2
  26.9 0.0 copy-done.2
  26.9 0.2 convolution_bitcast_fusion.5
  27.1 0.0 copy-done.1
  27.2 0.2 multiply_reduce_fusion.4
  27.4 40.9 %all-reduce.1 = (f32[384]{0:T(512)S(1)}, f32[384]{0:T(512)S(1)}) all-reduce(f32[384]{0:T(512)S(1)} %get-tuple-element.12, f32[384]{0:T(512)S(1)} %get-tuple-element.11), channel_id=1, replica_groups=mesh['blk'=4,'grp'=8] {'blk','grp'}, use_global_device_ids=true, to_apply=%region_1.0 | all-reduce | flops 768 | bytes 6144 | tf_op jit(solution)/shard_map/psum | solution.py:54
  68.3 0.1 multiply_reduce_fusion.3
  68.3 40.3 %psum.44 = f32[384]{0:T(512)S(1)} all-reduce(f32[384]{0:T(512)S(1)} %multiply_reduce_fusion.3), channel_id=1, replica_groups=mesh['blk'=4,'grp'=8] {'blk','grp'}, use_global_device_ids=true, to_apply=%region_5.0 | all-reduce | flops 384 | bytes 3072 | tf_op jit(solution)/shard_map/psum | solution.py:59
  108.7 1.9 fusion.11
  110.6 14.9 %all-gather.1 = bf16[512,384]{1,0:T(8,128)(2,1)S(1)} all-gather(bf16[128,384]{1,0:T(8,128)(2,1)S(1)} %get-tuple-element.20), channel_id=3, replica_groups=mesh['blk'=4,'grp'=8] {'blk'}, dimensions={0}, use_global_device_ids=true | all-gather | bytes 491520 | tf_op jit(solution)/shard_map/all_gather | solution.py:28
  125.6 0.1 reshape.90
  125.7 0.4 convolution_convert_fusion.1
  126.1 0.2 convolution_bitcast_fusion.3
  126.4 0.2 multiply_reduce_fusion.1
  126.6 39.9 %all-reduce = (f32[384]{0:T(512)S(1)}, f32[384]{0:T(512)S(1)}) all-reduce(f32[384]{0:T(512)S(1)} %get-tuple-element.10, f32[384]{0:T(512)S(1)} %get-tuple-element.9), channel_id=1, replica_groups=mesh['blk'=4,'grp'=8] {'blk','grp'}, use_global_device_ids=true, to_apply=%region_7.0 | all-reduce | flops 768 | bytes 6144 | tf_op jit(solution)/shard_map/psum | solution.py:54
  166.5 0.0 copy-start.3
  166.5 0.1 multiply_reduce_fusion
  166.5 40.4 %psum.47 = f32[384]{0:T(512)S(1)} all-reduce(f32[384]{0:T(512)S(1)} %multiply_reduce_fusion), channel_id=1, replica_groups=mesh['blk'=4,'grp'=8] {'blk','grp'}, use_global_device_ids=true, to_apply=%region_11.0 | all-reduce | flops 384 | bytes 3072 | tf_op jit(solution)/shard_map/psum | solution.py:59
  206.9 0.1 fusion.55
  207.0 18.3 %all-gather.2 = bf16[512,768]{1,0:T(8,128)(2,1)S(1)} all-gather(bf16[128,768]{1,0:T(8,128)(2,1)S(1)} %pad_maximum_fusion.2), channel_id=4, replica_groups=mesh['blk'=4,'grp'=8] {'blk'}, dimensions={0}, use_global_device_ids=true | all-gather | bytes 983040 | tf_op jit(solution)/shard_map/all_gather | solution.py:26
  225.3 0.6 reshape.93
  225.9 0.6 convolution_convert_fusion
  226.5 0.0 copy-done.3
  226.5 0.4 fusion.16
  226.9 0.4 fusion.17
  227.4 0.1 copy.19
  227.5 0.1 copy.20
  227.6 0.9 fusion
  228.5 0.9 fusion.1
  229.4 2.8 pad_maximum_fusion
  232.2 0.0 reduce-scatter.5.cloned.1.call-update
  232.3 0.0 reduce-scatter.7.cloned.1.call-start
  232.3 57.6 %reduce-scatter.5.cloned.1.call-done = bf16[144,2,1152]{2,0,1:T(8,128)(2,1)} async-done(((bf16[1152,2,1152]{2,0,1:T(8,128)(2,1)}), bf16[144,2,1152]{2,0,1:T(8,128)(2,1)}) %reduce-scatter.5.cloned.1.call-update) | async-done | bytes 663568 | tf_op jit(solution)/shard_map/reduce_scatter | solution.py:72
  289.9 3.5 %copy.28 = bf16[144,2,1152]{0,1,2:T(2,128)(2,1)S(1)} copy(bf16[144,2,1152]{2,0,1:T(8,128)(2,1)} %reduce-scatter.5.cloned.1.call-done) | data formatting | bytes 1327104
  293.4 1.5 reshape.107
  294.9 0.0 reduce-scatter.7.cloned.1.call-update
  295.0 0.7 fusion.54
  295.7 24.0 %reduce-scatter.7.cloned.1.call-done = bf16[288,288]{1,0:T(8,128)(2,1)} async-done(((bf16[1152,288]{1,0:T(8,128)(2,1)}), bf16[288,288]{1,0:T(8,128)(2,1)}) %reduce-scatter.7.cloned.1.call-update) | async-done | bytes 165904
  319.7 1.1 reshape.108
  320.8 0.2 copy.29
  321.0 0.9 copy.21
  (8 shorter events, 0.1 us)
Async XLA Ops:
  7.2 1.0 copy-start
  7.2 19.3 %copy-start.4 = (s32[1,1,4]{2,1,0:T(1,128)S(1)}, s32[1,1,4]{2,1,0:T(1,128)}, u32[]{:S(2)}) copy-start(s32[1,1,4]{2,1,0:T(1,128)} %param.9) | copy-start | bytes 52
  7.2 19.7 %copy-start.2 = (bf16[1,1,4,128,128]{4,3,2,1,0:T(8,128)(2,1)S(1)}, bf16[1,1,4,128,128]{4,3,2,1,0:T(8,128)(2,1)}, u32[]{:S(2)}) copy-start(bf16[1,1,4,128,128]{4,3,2,1,0:T(8,128)(2,1)} %param.7) | copy-start | bytes 393220
  7.2 19.9 %copy-start.1 = (bf16[1,1,4,128,128]{4,3,2,1,0:T(8,128)(2,1)S(1)}, bf16[1,1,4,128,128]{4,3,2,1,0:T(8,128)(2,1)}, u32[]{:S(2)}) copy-start(bf16[1,1,4,128,128]{4,3,2,1,0:T(8,128)(2,1)} %param.8) | copy-start | bytes 393220
  7.2 282.7 %reduce-scatter.5.cloned.1.call-start = ((), (), s32[]{:S(2)}) async-start(), calls=%async_computation.2 | async-start | bytes 5971968 | tf_op jit(solution)/shard_map/reduce_scatter | solution.py:72
  166.5 60.0 %copy-start.3 = (f32[384]{0:T(512)}, f32[384]{0:T(512)S(1)}, u32[]{:S(2)}) copy-start(f32[384]{0:T(512)S(1)} %add_divide_fusion) | copy-start | bytes 4612
  232.3 87.4 %reduce-scatter.7.cloned.1.call-start = ((), (), s32[]{:S(2)}) async-start(), calls=%async_computation.3 | async-start | bytes 1105920
Sparse Core Ops, SparseCore 0:
  232.4 57.4 reduce-scatter.4
  295.1 24.5 reduce-scatter.6
where the time goes:
time: 330 us; the launch traced here: 329 us
  blocking collectives  211 us (64%)
  waiting for transfers between devices  81.6 us (25%)
  between operations  14.3 us (4%)
  local copies, waits for them, and re-layouts  9.36 us (3%)
  matrix products  8.84 us (3%)
  other arithmetic  3.82 us (1%)
    psum x2, blocking collectives, body(): lax.psum((jnp.sum(stiff_x * mass_x, axis=0), jnp.sum(mass_x * mass_x, axi...  80.8 us
    psum x2, blocking collectives, body(): resid_sum = lax.psum(jnp.sum(residual * residual, axis=0), ('blk', 'grp'))  80.7 us
    reduce_scatter x1, waiting for transfers between devices, body(): lax.psum_scatter(jnp.stack([gram_stiff, gram_mass], axis=1).astype(jnp.bf...  57.6 us
    all_gather x3, blocking collectives, apply_pair(): lax.all_gather(own_blocks, 'blk', axis=0, tiled=True)  49.4 us
    unnamed x3, waiting for transfers between devices  24 us
    unnamed x15, local copies, waits for them, and re-layouts  8.2 us
  transfers between devices with their start and end apart: 2, of which 2 were waited for; matrix products, arithmetic and copies ran while one was open for 0% of the time, Pallas kernels for 0%

commit v1 on v0

--- a/solution.py
+++ b/solution.py
@@ -56,7 +56,9 @@
         )
         ritz_value = numerator / (denominator + epsilon)
         residual = stiff_x - ritz_value * mass_x
-        resid_sum = lax.psum(jnp.sum(residual * residual, axis=0), ("blk", "grp"))
+        resid_sum = jnp.sum(residual * residual, axis=0)
+        for d in ("grp", "blk"):
+            resid_sum = lax.psum(resid_sum, d)
         next_search = (residual * lax.rsqrt(resid_sum / total_rows + epsilon)).astype(jnp.bfloat16)
         current = jnp.concatenate([next_modes, next_search, next_history], axis=1)
     stiff_rest, mass_rest = apply_pair(stiff, mass, cols, current[:, mode_count:], True)

time: 330 us -> 288 us (0.87)
  blocking collectives: 211 us -> 171 us
    psum x2 -> x4, blocking collectives: 80.7 us -> 46 us  [body(): resid_sum = lax.psum(resid_sum, d)]
where the time goes in v1:
time: 288 us
  blocking collectives  171 us (59%)
  waiting for transfers between devices  79.8 us (28%)
  between operations  14.3 us (5%)
  local copies, waits for them, and re-layouts  9.37 us (3%)
  matrix products  8.84 us (3%)
  other arithmetic  3.83 us (1%)
    psum x2, blocking collectives, body(): lax.psum((jnp.sum(stiff_x * mass_x, axis=0), jnp.sum(mass_x * mass_x, axi...  78.6 us
    reduce_scatter x1, waiting for transfers between devices, body(): lax.psum_scatter(jnp.stack([gram_stiff, gram_mass], axis=1).astype(jnp.bf...  55.7 us
    all_gather x3, blocking collectives, apply_pair(): lax.all_gather(own_blocks, 'blk', axis=0, tiled=True)  46.9 us
    psum x4, blocking collectives, body(): resid_sum = lax.psum(resid_sum, d)  46 us
    unnamed x3, waiting for transfers between devices  24 us
    unnamed x15, local copies, waits for them, and re-layouts  8.2 us
  transfers between devices with their start and end apart: 2, of which 2 were waited for; matrix products, arithmetic and copies ran while one was open for 0% of the time, Pallas kernels for 0%

profile of v1, /device:TPU:0, one launch (start us, length us, event | category | flops | bytes accessed | tf_op | source)
XLA Modules:
  0.0 287.6 jit_solution(11074586643223772297)
XLA Ops:
  7.2 0.0 copy-start
  7.2 0.0 copy-start.4
  7.2 0.0 copy-start.2
  7.2 0.0 copy-start.1
  7.2 0.0 reduce-scatter.5.cloned.1.call-start
  7.3 0.9 copy-done
  8.1 1.9 fusion.8
  10.1 16.2 %all-gather = bf16[512,384]{1,0:T(8,128)(2,1)S(1)} all-gather(bf16[128,384]{1,0:T(8,128)(2,1)S(1)} %get-tuple-element.22), channel_id=2, replica_groups=mesh['blk'=4,'grp'=8] {'blk'}, dimensions={0}, use_global_device_ids=true | all-gather | bytes 491520 | tf_op jit(solution)/shard_map/all_gather | solution.py:28
  26.3 0.1 reshape.85
  26.5 0.0 copy-done.4
  26.5 0.4 convolution_convert_fusion.2
  26.9 0.0 copy-done.2
  26.9 0.2 convolution_bitcast_fusion.5
  27.1 0.0 copy-done.1
  27.2 0.2 multiply_reduce_fusion.4
  27.4 40.9 %all-reduce.1 = (f32[384]{0:T(512)S(1)}, f32[384]{0:T(512)S(1)}) all-reduce(f32[384]{0:T(512)S(1)} %get-tuple-element.12, f32[384]{0:T(512)S(1)} %get-tuple-element.11), channel_id=1, replica_groups=mesh['blk'=4,'grp'=8] {'blk','grp'}, use_global_device_ids=true, to_apply=%region_1.0 | all-reduce | flops 768 | bytes 6144 | tf_op jit(solution)/shard_map/psum | solution.py:54
  68.3 0.1 multiply_reduce_fusion.3
  68.3 12.7 %psum.58 = f32[384]{0:T(512)S(1)} all-reduce(f32[384]{0:T(512)S(1)} %multiply_reduce_fusion.3), channel_id=1, replica_groups=mesh['blk'=4,'grp'=8] {'grp'}, use_global_device_ids=true, to_apply=%region_5.0 | all-reduce | flops 384 | bytes 3072 | tf_op jit(solution)/shard_map/psum | solution.py:61
  81.0 10.0 %psum.59 = f32[384]{0:T(512)S(1)} all-reduce(f32[384]{0:T(512)S(1)} %psum.58), channel_id=1, replica_groups=mesh['blk'=4,'grp'=8] {'blk'}, use_global_device_ids=true, to_apply=%region_6.0 | all-reduce | flops 384 | bytes 3072 | tf_op jit(solution)/shard_map/psum | solution.py:61
  91.1 1.9 fusion.11
  93.1 14.2 %all-gather.1 = bf16[512,384]{1,0:T(8,128)(2,1)S(1)} all-gather(bf16[128,384]{1,0:T(8,128)(2,1)S(1)} %get-tuple-element.20), channel_id=3, replica_groups=mesh['blk'=4,'grp'=8] {'blk'}, dimensions={0}, use_global_device_ids=true | all-gather | bytes 491520 | tf_op jit(solution)/shard_map/all_gather | solution.py:28
  107.3 0.1 reshape.90
  107.5 0.4 convolution_convert_fusion.1
  107.9 0.2 convolution_bitcast_fusion.3
  108.1 0.2 multiply_reduce_fusion.1
  108.4 37.7 %all-reduce = (f32[384]{0:T(512)S(1)}, f32[384]{0:T(512)S(1)}) all-reduce(f32[384]{0:T(512)S(1)} %get-tuple-element.10, f32[384]{0:T(512)S(1)} %get-tuple-element.9), channel_id=1, replica_groups=mesh['blk'=4,'grp'=8] {'blk','grp'}, use_global_device_ids=true, to_apply=%region_8.0 | all-reduce | flops 768 | bytes 6144 | tf_op jit(solution)/shard_map/psum | solution.py:54
  146.0 0.0 copy-start.3
  146.0 0.1 multiply_reduce_fusion
  146.1 12.7 %psum.62 = f32[384]{0:T(512)S(1)} all-reduce(f32[384]{0:T(512)S(1)} %multiply_reduce_fusion), channel_id=1, replica_groups=mesh['blk'=4,'grp'=8] {'grp'}, use_global_device_ids=true, to_apply=%region_12.0 | all-reduce | flops 384 | bytes 3072 | tf_op jit(solution)/shard_map/psum | solution.py:61
  158.8 10.6 %psum.63 = f32[384]{0:T(512)S(1)} all-reduce(f32[384]{0:T(512)S(1)} %psum.62), channel_id=1, replica_groups=mesh['blk'=4,'grp'=8] {'blk'}, use_global_device_ids=true, to_apply=%region_13.0 | all-reduce | flops 384 | bytes 3072 | tf_op jit(solution)/shard_map/psum | solution.py:61
  169.4 0.1 fusion.55
  169.5 16.5 %all-gather.2 = bf16[512,768]{1,0:T(8,128)(2,1)S(1)} all-gather(bf16[128,768]{1,0:T(8,128)(2,1)S(1)} %pad_maximum_fusion.2), channel_id=4, replica_groups=mesh['blk'=4,'grp'=8] {'blk'}, dimensions={0}, use_global_device_ids=true | all-gather | bytes 983040 | tf_op jit(solution)/shard_map/all_gather | solution.py:26
  185.9 0.6 reshape.93
  186.5 0.6 convolution_convert_fusion
  187.1 0.0 copy-done.3
  187.1 0.4 fusion.16
  187.6 0.4 fusion.17
  188.0 0.1 copy.19
  188.1 0.1 copy.20
  188.3 0.9 fusion
  189.1 0.9 fusion.1
  190.0 2.8 pad_maximum_fusion
  192.9 0.0 reduce-scatter.5.cloned.1.call-update
  192.9 0.0 reduce-scatter.7.cloned.1.call-start
  193.0 55.7 %reduce-scatter.5.cloned.1.call-done = bf16[144,2,1152]{2,0,1:T(8,128)(2,1)} async-done(((bf16[1152,2,1152]{2,0,1:T(8,128)(2,1)}), bf16[144,2,1152]{2,0,1:T(8,128)(2,1)}) %reduce-scatter.5.cloned.1.call-update) | async-done | bytes 663568 | tf_op jit(solution)/shard_map/reduce_scatter | solution.py:74
  248.7 3.5 %copy.28 = bf16[144,2,1152]{0,1,2:T(2,128)(2,1)S(1)} copy(bf16[144,2,1152]{2,0,1:T(8,128)(2,1)} %reduce-scatter.5.cloned.1.call-done) | data formatting | bytes 1327104
  252.2 1.5 reshape.107
  253.7 0.0 reduce-scatter.7.cloned.1.call-update
  253.8 0.7 fusion.54
  254.5 24.0 %reduce-scatter.7.cloned.1.call-done = bf16[288,288]{1,0:T(8,128)(2,1)} async-done(((bf16[1152,288]{1,0:T(8,128)(2,1)}), bf16[288,288]{1,0:T(8,128)(2,1)}) %reduce-scatter.7.cloned.1.call-update) | async-done | bytes 165904
  278.5 1.1 reshape.108
  279.6 0.2 copy.29
  279.8 0.9 copy.21
  (8 shorter events, 0.1 us)
Async XLA Ops:
  7.2 1.0 copy-start
  7.2 19.3 %copy-start.4 = (s32[1,1,4]{2,1,0:T(1,128)S(1)}, s32[1,1,4]{2,1,0:T(1,128)}, u32[]{:S(2)}) copy-start(s32[1,1,4]{2,1,0:T(1,128)} %param.9) | copy-start | bytes 52
  7.2 19.7 %copy-start.2 = (bf16[1,1,4,128,128]{4,3,2,1,0:T(8,128)(2,1)S(1)}, bf16[1,1,4,128,128]{4,3,2,1,0:T(8,128)(2,1)}, u32[]{:S(2)}) copy-start(bf16[1,1,4,128,128]{4,3,2,1,0:T(8,128)(2,1)} %param.7) | copy-start | bytes 393220
  7.2 19.9 %copy-start.1 = (bf16[1,1,4,128,128]{4,3,2,1,0:T(8,128)(2,1)S(1)}, bf16[1,1,4,128,128]{4,3,2,1,0:T(8,128)(2,1)}, u32[]{:S(2)}) copy-start(bf16[1,1,4,128,128]{4,3,2,1,0:T(8,128)(2,1)} %param.8) | copy-start | bytes 393220
  7.2 241.5 %reduce-scatter.5.cloned.1.call-start = ((), (), s32[]{:S(2)}) async-start(), calls=%async_computation.2 | async-start | bytes 5971968 | tf_op jit(solution)/shard_map/reduce_scatter | solution.py:74
  146.0 41.1 %copy-start.3 = (f32[384]{0:T(512)}, f32[384]{0:T(512)S(1)}, u32[]{:S(2)}) copy-start(f32[384]{0:T(512)S(1)} %add_divide_fusion) | copy-start | bytes 4612
  192.9 85.6 %reduce-scatter.7.cloned.1.call-start = ((), (), s32[]{:S(2)}) async-start(), calls=%async_computation.3 | async-start | bytes 1105920
Sparse Core Ops, SparseCore 0:
  193.0 55.6 reduce-scatter.4
  253.9 24.5 reduce-scatter.6
